TPU v7x, 32 devices: a whole 2x2x4 slice. The times are simulated.
32 devices in a mesh: segment: 8 (over y, x, core), rows: 4 (over z).
Axes of the slice: x: 2, y: 2, z: 4, core: 2. Of those that a mesh axis runs over, the one named last changes fastest.
Arguments:
- held_maps: bfloat16 [8, 64, 64, 256], P('segment', 'rows'), may hold values from -6 to 6
- held_skips: bfloat16 [3, 8, 64, 64, 256], P(None, 'segment', 'rows'), may hold values from -6 to 6
- arrivals: bfloat16 [3, 64, 64, 256], P(None, 'rows'), may hold values from -6 to 6
- kernels: bfloat16 [8, 3, 3, 768, 256], P('segment'), may hold values from -0.125 to 0.125
- biases: float32 [8, 3, 256], P('segment'), may hold values from -3 to 3
Outputs:
- section_maps: bfloat16 [3, 8, 64, 64, 256], P(None, 'segment', 'rows')
- skip_stash: bfloat16 [3, 8, 64, 64, 256], P(None, 'segment', 'rows')
All inputs are finite; a program needn't handle non-finite values.
Results may differ from a plain program's by a relative error of at most 0.0075.
Values may be sent and summed in bfloat16 or wider, within the bound.
A program may use at most 64 MiB of HBM per device.

v0:
```python
import jax
import jax.numpy as jnp
from jax import lax
from jax.sharding import PartitionSpec as P

TICKS = 3


def with_halo(block, sides, width):
    for axis, dim in sides:
        count = lax.axis_size(axis)
        forward = [(i, i + 1) for i in range(count - 1)]
        backward = [(target, source) for source, target in forward]
        low = lax.ppermute(
            lax.slice_in_dim(block, block.shape[dim] - width, None, axis=dim), axis, forward
        )
        high = lax.ppermute(lax.slice_in_dim(block, 0, width, axis=dim), axis, backward)
        block = jnp.concatenate([low, block, high], axis=dim)
    return block


def shifted(x, axis, by):
    length = lax.axis_size(axis)
    pairs = [(i, i + by) for i in range(length) if 0 <= i + by < length]
    return lax.ppermute(x, axis, pairs)


def swapped(value, axis, stride):
    mask = 2**stride
    pairs = [(source, source ^ mask) for source in range(lax.axis_size(axis))]
    return lax.ppermute(value, axis, pairs)


def convolve(source, kernel, offsets):
    rows_out = source.shape[0] - 2
    columns_count = source.shape[1]
    padded = jnp.pad(source, ((0, 0), (1, 1), (0, 0)))
    columns = jnp.concatenate(
        [
            padded[:, 0:columns_count],
            padded[:, 1 : columns_count + 1],
            padded[:, 2 : columns_count + 2],
        ],
        axis=-1,
    )
    summed = jnp.zeros((rows_out * columns_count, kernel.shape[2]), jnp.float32)
    for row_offset in range(3):
        block = columns[row_offset : row_offset + rows_out].reshape(rows_out * columns_count, -1)
        summed = summed + jnp.dot(block, kernel[row_offset], preferred_element_type=jnp.float32)
    return summed.reshape(rows_out, columns_count, -1) + offsets


def run_section(section_in, kernel, offsets):
    local_rows = section_in.shape[0]
    total_rows = local_rows * lax.axis_size("rows")
    row_start = lax.axis_index("rows") * local_rows
    widened = with_halo(section_in, (("rows", 0),), 3)
    hidden_state = widened
    for layer_index in range(2):
        margin = 2 - layer_index
        global_rows = row_start - margin + jnp.arange(local_rows + 2 * margin, dtype=jnp.int32)
        inside = ((global_rows >= 0) & (global_rows < total_rows))[:, None, None]
        activated = jax.nn.silu(convolve(hidden_state, kernel[layer_index], offsets[layer_index]))
        hidden_state = jnp.where(inside, activated, 0.0).astype(jnp.bfloat16)
    summed = section_in.astype(jnp.float32) + convolve(hidden_state, kernel[2], offsets[2])
    return summed.astype(jnp.bfloat16)


def on_device(held_maps, held_skips, arrivals, kernels, biases):
    segment_count = lax.axis_size("segment")
    segment_index = lax.axis_index("segment")
    kernel = kernels[0]
    offsets = biases[0]
    previous = held_maps[0]
    decoder_enabled = segment_index >= segment_count // 2
    is_middle = segment_index == segment_count // 2
    section_results = []
    stored_skips = []
    for tick in range(TICKS):
        passed_along = shifted(previous, "segment", 1)
        incoming = jnp.where(segment_index == 0, arrivals[tick], passed_along)
        if tick >= 1:
            skip = jnp.where(is_middle, passed_along, held_skips[tick, 0])
        else:
            skip = held_skips[tick, 0]
        joined = (incoming.astype(jnp.float32) + skip.astype(jnp.float32)).astype(jnp.bfloat16)
        section_in = jnp.where(decoder_enabled, joined, incoming)
        new_activation = run_section(section_in, kernel, offsets)
        section_results.append(new_activation)
        mirrored_skip = new_activation
        for bit_number in range(segment_count.bit_length() - 1):
            mirrored_skip = swapped(mirrored_skip, "segment", bit_number)
        stored_skips.append(
            jnp.where(decoder_enabled, mirrored_skip, jnp.zeros_like(mirrored_skip))
        )
        previous = new_activation
    return (jnp.stack(section_results)[:, None], jnp.stack(stored_skips)[:, None])


def solution(mesh):
    placed = (
        P("segment", "rows", None, None),
        P(None, "segment", "rows", None, None),
        P(None, "rows", None, None),
        P("segment", None, None, None, None),
        P("segment", None, None),
    )
    return jax.shard_map(
        on_device,
        mesh=mesh,
        in_specs=placed,
        out_specs=(P(None, "segment", "rows", None, None), P(None, "segment", "rows", None, None)),
        check_vma=False,
    )
```

profile of v0, /device:TPU:0, one launch (start us, length us, event | category | flops | bytes accessed | tf_op | source)
XLA Modules:
  0.0 157.7 jit_solution(3112354016297140581)
XLA Ops:
  0.6 2.4 %collective-permute-start = (bf16[16,64,256]{2,1,0:T(8,128)(2,1)}, bf16[16,64,256]{2,1,0:T(8,128)(2,1)S(1)}, u32[]{:S(2)}, u32[]{:S(2)}) collective-permute-start(bf16[16,64,256]{2,1,0:T(8,128)(2,1)} %bitcast.213), channel_id=1, source_target_pairs={{0,4},{4,8},{8,12},{12,16},{16,20},{20,24},{24,28},{1,5},{5,9},{9,... | collective-permute-start | bytes 1572872 | tf_op jit(solution)/shard_map/ppermute | solution.py:25
  3.1 0.7 fusion.83
  3.8 0.9 collective-permute-done
  4.8 1.5 fusion.4
  6.2 4.3 %collective-permute-start.1 = (bf16[3,64,256]{2,1,0:T(8,128)(2,1)S(1)}, bf16[3,64,256]{2,1,0:T(8,128)(2,1)S(1)}, u32[]{:S(2)}, u32[]{:S(2)}) collective-permute-start(bf16[3,64,256]{2,1,0:T(8,128)(2,1)S(1)} %get-tuple-element.51), channel_id=1, source_target_pairs={{0,1},{1,2},{2,3},{4,5},{5,6},{6,7},{8,9},{9,10},{10,11},{12,13},{... | collective-permute-start | bytes 294920 | tf_op jit(solution)/shard_map/ppermute | solution.py:14
  10.6 1.3 collective-permute-start.2
  11.9 0.9 collective-permute-done.1
  12.7 4.3 %collective-permute-done.2 = bf16[3,64,256]{2,1,0:T(8,128)(2,1)S(1)} collective-permute-done((bf16[3,64,256]{2,1,0:T(8,128)(2,1)S(1)}, bf16[3,64,256]{2,1,0:T(8,128)(2,1)S(1)}, u32[]{:S(2)}, u32[]{:S(2)}) %collective-permute-start.2) | collective-permute-done | bytes 98336 | tf_op jit(solution)/shard_map/ppermute | solution.py:17
  18.2 0.7 fusion.70
  18.9 1.3 copy-done
  20.2 0.7 fusion.39
  20.9 0.7 convolution_add_fusion.11
  21.6 0.7 convolution_add_fusion.10
  23.3 0.6 fusion.73
  23.9 0.6 fusion.27
  24.6 0.6 convolution_add_fusion.5
  25.2 0.6 convolution_add_fusion.4
  27.3 0.6 fusion.15
  27.9 0.6 convolution_add_fusion.17
  28.5 0.6 convolution_add_fusion.16
  29.0 1.0 add_convert_fusion.4
  30.0 7.7 %collective-permute-start.3 = (bf16[16,64,256]{2,1,0:T(8,128)(2,1)}, bf16[16,64,256]{2,1,0:T(8,128)(2,1)}, u32[]{:S(2)}, u32[]{:S(2)}) collective-permute-start(bf16[16,64,256]{2,1,0:T(8,128)(2,1)} %add_convert_fusion.4), channel_id=1, source_target_pairs={{0,4},{4,8},{8,12},{12,16},{16,20},{20,24},{24,28},{1,5},{5,9},{9,... | collective-permute-start | bytes 1572872 | tf_op jit(solution)/shard_map/ppermute | solution.py:25
  37.8 1.1 collective-permute-done.3
  38.8 1.6 %fusion.2 = bf16[16,64,256]{2,1,0:T(8,128)(2,1)S(1)} fusion(bf16[16,64,256]{2,1,0:T(8,128)(2,1)} %collective-permute-done.3, bf16[3,1,16,64,256]{4,3,2,1,0:T(8,128)(2,1)} %param.6, bf16[3,16,64,256]{3,2,1,0:T(8,128)(2,1)} %param.7, pred[]{:T(512)S(6)} %eq.9, pred[]{:T(512)S(6)} %eq.8, pred[]{:T(512)S(6)} %ge.21), kind=kLoop, calls=%fused_computation.51 | loop fusion | flops 1835008 | bytes 2097155 | tf_op jit(solution)/shard_map/jit(_where)/select_n | solution.py:87
  40.5 3.5 %collective-permute-start.4 = (bf16[3,64,256]{2,1,0:T(8,128)(2,1)S(1)}, bf16[3,64,256]{2,1,0:T(8,128)(2,1)S(1)}, u32[]{:S(2)}, u32[]{:S(2)}) collective-permute-start(bf16[3,64,256]{2,1,0:T(8,128)(2,1)S(1)} %get-tuple-element.49), channel_id=1, source_target_pairs={{0,1},{1,2},{2,3},{4,5},{5,6},{6,7},{8,9},{9,10},{10,11},{12,13},{... | collective-permute-start | bytes 294920 | tf_op jit(solution)/shard_map/ppermute | solution.py:14
  44.0 1.5 collective-permute-start.5
  45.5 0.7 collective-permute-done.4
  46.2 4.3 %collective-permute-done.5 = bf16[3,64,256]{2,1,0:T(8,128)(2,1)S(1)} collective-permute-done((bf16[3,64,256]{2,1,0:T(8,128)(2,1)S(1)}, bf16[3,64,256]{2,1,0:T(8,128)(2,1)S(1)}, u32[]{:S(2)}, u32[]{:S(2)}) %collective-permute-start.5) | collective-permute-done | bytes 98336 | tf_op jit(solution)/shard_map/ppermute | solution.py:17
  51.6 0.7 fusion.69
  52.3 0.7 fusion.37
  53.0 0.7 convolution_add_fusion.9
  53.7 0.7 convolution_add_fusion.8
  55.4 0.6 fusion.72
  56.1 0.6 fusion.25
  56.7 0.6 convolution_add_fusion.3
  57.4 0.6 convolution_add_fusion.2
  59.4 0.6 fusion.13
  60.0 0.6 convolution_add_fusion.15
  61.4 8.9 %collective-permute-start.6 = (bf16[16,64,256]{2,1,0:T(8,128)(2,1)S(1)}, bf16[16,64,256]{2,1,0:T(8,128)(2,1)S(1)}, u32[]{:S(2)}, u32[]{:S(2)}) collective-permute-start(bf16[16,64,256]{2,1,0:T(8,128)(2,1)S(1)} %add_convert_fusion.2), channel_id=1, source_target_pairs={{0,4},{4,8},{8,12},{12,16},{16,20},{20,24},{24,28},{1,5},{5,9},{9,... | collective-permute-start | bytes 1572872 | tf_op jit(solution)/shard_map/ppermute | solution.py:25
  70.3 1.5 collective-permute-done.6
  71.8 1.5 fusion.3
  73.3 3.5 %collective-permute-start.7 = (bf16[3,64,256]{2,1,0:T(8,128)(2,1)S(1)}, bf16[3,64,256]{2,1,0:T(8,128)(2,1)S(1)}, u32[]{:S(2)}, u32[]{:S(2)}) collective-permute-start(bf16[3,64,256]{2,1,0:T(8,128)(2,1)S(1)} %get-tuple-element.47), channel_id=1, source_target_pairs={{0,1},{1,2},{2,3},{4,5},{5,6},{6,7},{8,9},{9,10},{10,11},{12,13},{... | collective-permute-start | bytes 294920 | tf_op jit(solution)/shard_map/ppermute | solution.py:14
  76.8 1.5 collective-permute-start.8
  78.3 8.3 %collective-permute-start.9 = (bf16[16,64,256]{2,1,0:T(8,128)(2,1)}, bf16[16,64,256]{2,1,0:T(8,128)(2,1)S(1)}, u32[]{:S(2)}, u32[]{:S(2)}) collective-permute-start(bf16[16,64,256]{2,1,0:T(8,128)(2,1)} %add_convert_fusion.4), channel_id=1, source_target_pairs={{0,4},{4,0},{8,12},{12,8},{16,20},{20,16},{24,28},{28,24},{1,5},{5... | collective-permute-start | bytes 1572872 | tf_op jit(solution)/shard_map/ppermute | solution.py:31
  87.8 0.7 fusion.68
  88.5 0.7 fusion.35
  89.2 0.7 convolution_add_fusion.7
  89.9 0.7 convolution_add_fusion.6
  91.6 0.6 fusion.71
  92.2 0.6 fusion.23
  92.9 0.6 convolution_add_fusion.1
  93.5 0.6 convolution_add_fusion
  97.6 3.8 %collective-permute-start.15 = (bf16[16,64,256]{2,1,0:T(8,128)(2,1)S(1)}, bf16[16,64,256]{2,1,0:T(8,128)(2,1)S(1)}, u32[]{:S(2)}, u32[]{:S(2)}) collective-permute-start(bf16[16,64,256]{2,1,0:T(8,128)(2,1)S(1)} %add_convert_fusion), channel_id=1, source_target_pairs={{0,4},{4,0},{8,12},{12,8},{16,20},{20,16},{24,28},{28,24},{1,5},{5... | collective-permute-start | bytes 1572872 | tf_op jit(solution)/shard_map/ppermute | solution.py:31
  101.3 4.6 %collective-permute-start.10 = (bf16[16,64,256]{2,1,0:T(8,128)(2,1)S(1)}, bf16[16,64,256]{2,1,0:T(8,128)(2,1)S(1)}, u32[]{:S(2)}, u32[]{:S(2)}) collective-permute-start(bf16[16,64,256]{2,1,0:T(8,128)(2,1)S(1)} %collective-permute-done.9), channel_id=1, source_target_pairs={{0,8},{4,12},{8,0},{12,4},{16,24},{20,28},{24,16},{28,20},{1,9},{5... | collective-permute-start | bytes 1572872 | tf_op jit(solution)/shard_map/ppermute | solution.py:31
  106.0 1.9 %collective-permute-start.16 = (bf16[16,64,256]{2,1,0:T(8,128)(2,1)S(1)}, bf16[16,64,256]{2,1,0:T(8,128)(2,1)S(1)}, u32[]{:S(2)}, u32[]{:S(2)}) collective-permute-start(bf16[16,64,256]{2,1,0:T(8,128)(2,1)S(1)} %collective-permute-done.15), channel_id=1, source_target_pairs={{0,8},{4,12},{8,0},{12,4},{16,24},{20,28},{24,16},{28,20},{1,9},{5... | collective-permute-start | bytes 1572872 | tf_op jit(solution)/shard_map/ppermute | solution.py:31
  108.0 10.7 %collective-permute-done.10 = bf16[16,64,256]{2,1,0:T(8,128)(2,1)S(1)} collective-permute-done((bf16[16,64,256]{2,1,0:T(8,128)(2,1)S(1)}, bf16[16,64,256]{2,1,0:T(8,128)(2,1)S(1)}, u32[]{:S(2)}, u32[]{:S(2)}) %collective-permute-start.10) | collective-permute-done | bytes 524320 | tf_op jit(solution)/shard_map/ppermute | solution.py:31
  118.7 4.0 %collective-permute-start.11 = (bf16[16,64,256]{2,1,0:T(8,128)(2,1)S(1)}, bf16[16,64,256]{2,1,0:T(8,128)(2,1)S(1)}, u32[]{:S(2)}, u32[]{:S(2)}) collective-permute-start(bf16[16,64,256]{2,1,0:T(8,128)(2,1)S(1)} %collective-permute-done.10), channel_id=1, source_target_pairs={{0,16},{4,20},{8,24},{12,28},{16,0},{20,4},{24,8},{28,12},{1,17},{... | collective-permute-start | bytes 1572872 | tf_op jit(solution)/shard_map/ppermute | solution.py:31
  122.7 7.2 %collective-permute-done.13 = bf16[16,64,256]{2,1,0:T(8,128)(2,1)S(1)} collective-permute-done((bf16[16,64,256]{2,1,0:T(8,128)(2,1)S(1)}, bf16[16,64,256]{2,1,0:T(8,128)(2,1)S(1)}, u32[]{:S(2)}, u32[]{:S(2)}) %collective-permute-start.13) | collective-permute-done | bytes 524320 | tf_op jit(solution)/shard_map/ppermute | solution.py:31
  129.9 4.0 %collective-permute-start.14 = (bf16[16,64,256]{2,1,0:T(8,128)(2,1)S(1)}, bf16[16,64,256]{2,1,0:T(8,128)(2,1)S(1)}, u32[]{:S(2)}, u32[]{:S(2)}) collective-permute-start(bf16[16,64,256]{2,1,0:T(8,128)(2,1)S(1)} %collective-permute-done.13), channel_id=1, source_target_pairs={{0,16},{4,20},{8,24},{12,28},{16,0},{20,4},{24,8},{28,12},{1,17},{... | collective-permute-start | bytes 1572872 | tf_op jit(solution)/shard_map/ppermute | solution.py:31
  134.0 6.9 %collective-permute-done.16 = bf16[16,64,256]{2,1,0:T(8,128)(2,1)S(1)} collective-permute-done((bf16[16,64,256]{2,1,0:T(8,128)(2,1)S(1)}, bf16[16,64,256]{2,1,0:T(8,128)(2,1)S(1)}, u32[]{:S(2)}, u32[]{:S(2)}) %collective-permute-start.16) | collective-permute-done | bytes 524320 | tf_op jit(solution)/shard_map/ppermute | solution.py:31
  140.9 3.7 %collective-permute-start.17 = (bf16[16,64,256]{2,1,0:T(8,128)(2,1)S(1)}, bf16[16,64,256]{2,1,0:T(8,128)(2,1)S(1)}, u32[]{:S(2)}, u32[]{:S(2)}) collective-permute-start(bf16[16,64,256]{2,1,0:T(8,128)(2,1)S(1)} %collective-permute-done.16), channel_id=1, source_target_pairs={{0,16},{4,20},{8,24},{12,28},{16,0},{20,4},{24,8},{28,12},{1,17},{... | collective-permute-start | bytes 1572872 | tf_op jit(solution)/shard_map/ppermute | solution.py:31
  144.6 2.4 %maximum_bitcast_fusion = bf16[3,1,16,64,256]{4,3,2,1,0:T(8,128)(2,1)} fusion(bf16[1,16,64,256]{3,2,1,0:T(8,128)(2,1)S(1)} %bitcast.203, bf16[1,16,64,256]{3,2,1,0:T(8,128)(2,1)S(1)} %bitcast.202, bf16[1,16,64,256]{3,2,1,0:T(8,128)(2,1)} %bitcast.27), kind=kLoop, calls=%fused_computation.24 | loop fusion | flops 1572864 | bytes 3145728 | tf_op jit(solution)/shard_map/broadcast_in_dim | solution.py:97
  147.1 9.2 %collective-permute-done.17 = bf16[16,64,256]{2,1,0:T(8,128)(2,1)S(1)} collective-permute-done((bf16[16,64,256]{2,1,0:T(8,128)(2,1)S(1)}, bf16[16,64,256]{2,1,0:T(8,128)(2,1)S(1)}, u32[]{:S(2)}, u32[]{:S(2)}) %collective-permute-start.17) | collective-permute-done | bytes 524320 | tf_op jit(solution)/shard_map/ppermute | solution.py:31
  156.3 1.3 maximum_bitcast_fusion.1
  (58 shorter events, 13.7 us)
Async XLA Ops:
  0.6 4.1 %collective-permute-start = (bf16[16,64,256]{2,1,0:T(8,128)(2,1)}, bf16[16,64,256]{2,1,0:T(8,128)(2,1)S(1)}, u32[]{:S(2)}, u32[]{:S(2)}) collective-permute-start(bf16[16,64,256]{2,1,0:T(8,128)(2,1)} %bitcast.213), channel_id=1, source_target_pairs={{0,4},{4,8},{8,12},{12,16},{16,20},{20,24},{24,28},{1,5},{5,9},{9,... | collective-permute-start | bytes 1572872 | tf_op jit(solution)/shard_map/ppermute | solution.py:25
  3.1 19.2 %copy-start.1 = (pred[20]{0:T(512)(128)(4,1)}, pred[20]{0:T(512)(128)(4,1)S(1)}, u32[]{:S(2)}) copy-start(pred[20]{0:T(512)(128)(4,1)S(1)} %compare_and_fusion) | copy-start | bytes 64
  6.2 6.5 %collective-permute-start.1 = (bf16[3,64,256]{2,1,0:T(8,128)(2,1)S(1)}, bf16[3,64,256]{2,1,0:T(8,128)(2,1)S(1)}, u32[]{:S(2)}, u32[]{:S(2)}) collective-permute-start(bf16[3,64,256]{2,1,0:T(8,128)(2,1)S(1)} %get-tuple-element.51), channel_id=1, source_target_pairs={{0,1},{1,2},{2,3},{4,5},{5,6},{6,7},{8,9},{9,10},{10,11},{12,13},{... | collective-permute-start | bytes 294920 | tf_op jit(solution)/shard_map/ppermute | solution.py:14
  10.6 6.5 %collective-permute-start.2 = (bf16[3,64,256]{2,1,0:T(8,128)(2,1)S(1)}, bf16[3,64,256]{2,1,0:T(8,128)(2,1)S(1)}, u32[]{:S(2)}, u32[]{:S(2)}) collective-permute-start(bf16[3,64,256]{2,1,0:T(8,128)(2,1)S(1)} %get-tuple-element.52), channel_id=1, source_target_pairs={{1,0},{2,1},{3,2},{5,4},{6,5},{7,6},{9,8},{10,9},{11,10},{13,12},{... | collective-permute-start | bytes 294920 | tf_op jit(solution)/shard_map/ppermute | solution.py:17
  18.2 2.0 %copy-start = (bf16[1,3,3,768,256]{4,3,2,1,0:T(8,128)(2,1)S(1)}, bf16[1,3,3,768,256]{4,3,2,1,0:T(8,128)(2,1)}, u32[]{:S(2)}) copy-start(bf16[1,3,3,768,256]{4,3,2,1,0:T(8,128)(2,1)} %param.8) | copy-start | bytes 10616836
  30.0 8.8 %collective-permute-start.3 = (bf16[16,64,256]{2,1,0:T(8,128)(2,1)}, bf16[16,64,256]{2,1,0:T(8,128)(2,1)}, u32[]{:S(2)}, u32[]{:S(2)}) collective-permute-start(bf16[16,64,256]{2,1,0:T(8,128)(2,1)} %add_convert_fusion.4), channel_id=1, source_target_pairs={{0,4},{4,8},{8,12},{12,16},{16,20},{20,24},{24,28},{1,5},{5,9},{9,... | collective-permute-start | bytes 1572872 | tf_op jit(solution)/shard_map/ppermute | solution.py:25
  40.5 5.7 %collective-permute-start.4 = (bf16[3,64,256]{2,1,0:T(8,128)(2,1)S(1)}, bf16[3,64,256]{2,1,0:T(8,128)(2,1)S(1)}, u32[]{:S(2)}, u32[]{:S(2)}) collective-permute-start(bf16[3,64,256]{2,1,0:T(8,128)(2,1)S(1)} %get-tuple-element.49), channel_id=1, source_target_pairs={{0,1},{1,2},{2,3},{4,5},{5,6},{6,7},{8,9},{9,10},{10,11},{12,13},{... | collective-permute-start | bytes 294920 | tf_op jit(solution)/shard_map/ppermute | solution.py:14
  44.0 6.5 %collective-permute-start.5 = (bf16[3,64,256]{2,1,0:T(8,128)(2,1)S(1)}, bf16[3,64,256]{2,1,0:T(8,128)(2,1)S(1)}, u32[]{:S(2)}, u32[]{:S(2)}) collective-permute-start(bf16[3,64,256]{2,1,0:T(8,128)(2,1)S(1)} %get-tuple-element.50), channel_id=1, source_target_pairs={{1,0},{2,1},{3,2},{5,4},{6,5},{7,6},{9,8},{10,9},{11,10},{13,12},{... | collective-permute-start | bytes 294920 | tf_op jit(solution)/shard_map/ppermute | solution.py:17
  53.7 0.7 copy-start.2
  61.4 10.4 %collective-permute-start.6 = (bf16[16,64,256]{2,1,0:T(8,128)(2,1)S(1)}, bf16[16,64,256]{2,1,0:T(8,128)(2,1)S(1)}, u32[]{:S(2)}, u32[]{:S(2)}) collective-permute-start(bf16[16,64,256]{2,1,0:T(8,128)(2,1)S(1)} %add_convert_fusion.2), channel_id=1, source_target_pairs={{0,4},{4,8},{8,12},{12,16},{16,20},{20,24},{24,28},{1,5},{5,9},{9,... | collective-permute-start | bytes 1572872 | tf_op jit(solution)/shard_map/ppermute | solution.py:25
  73.3 13.4 %collective-permute-start.7 = (bf16[3,64,256]{2,1,0:T(8,128)(2,1)S(1)}, bf16[3,64,256]{2,1,0:T(8,128)(2,1)S(1)}, u32[]{:S(2)}, u32[]{:S(2)}) collective-permute-start(bf16[3,64,256]{2,1,0:T(8,128)(2,1)S(1)} %get-tuple-element.47), channel_id=1, source_target_pairs={{0,1},{1,2},{2,3},{4,5},{5,6},{6,7},{8,9},{9,10},{10,11},{12,13},{... | collective-permute-start | bytes 294920 | tf_op jit(solution)/shard_map/ppermute | solution.py:14
  76.8 9.9 %collective-permute-start.8 = (bf16[3,64,256]{2,1,0:T(8,128)(2,1)S(1)}, bf16[3,64,256]{2,1,0:T(8,128)(2,1)S(1)}, u32[]{:S(2)}, u32[]{:S(2)}) collective-permute-start(bf16[3,64,256]{2,1,0:T(8,128)(2,1)S(1)} %get-tuple-element.48), channel_id=1, source_target_pairs={{1,0},{2,1},{3,2},{5,4},{6,5},{7,6},{9,8},{10,9},{11,10},{13,12},{... | collective-permute-start | bytes 294920 | tf_op jit(solution)/shard_map/ppermute | solution.py:17
  78.3 23.0 %collective-permute-start.9 = (bf16[16,64,256]{2,1,0:T(8,128)(2,1)}, bf16[16,64,256]{2,1,0:T(8,128)(2,1)S(1)}, u32[]{:S(2)}, u32[]{:S(2)}) collective-permute-start(bf16[16,64,256]{2,1,0:T(8,128)(2,1)} %add_convert_fusion.4), channel_id=1, source_target_pairs={{0,4},{4,0},{8,12},{12,8},{16,20},{20,16},{24,28},{28,24},{1,5},{5... | collective-permute-start | bytes 1572872 | tf_op jit(solution)/shard_map/ppermute | solution.py:31
  86.6 19.4 %collective-permute-start.12 = (bf16[16,64,256]{2,1,0:T(8,128)(2,1)S(1)}, bf16[16,64,256]{2,1,0:T(8,128)(2,1)S(1)}, u32[]{:S(2)}, u32[]{:S(2)}) collective-permute-start(bf16[16,64,256]{2,1,0:T(8,128)(2,1)S(1)} %add_convert_fusion.2), channel_id=1, source_target_pairs={{0,4},{4,0},{8,12},{12,8},{16,20},{20,16},{24,28},{28,24},{1,5},{5... | collective-permute-start | bytes 1572872 | tf_op jit(solution)/shard_map/ppermute | solution.py:31
  97.6 8.5 %collective-permute-start.15 = (bf16[16,64,256]{2,1,0:T(8,128)(2,1)S(1)}, bf16[16,64,256]{2,1,0:T(8,128)(2,1)S(1)}, u32[]{:S(2)}, u32[]{:S(2)}) collective-permute-start(bf16[16,64,256]{2,1,0:T(8,128)(2,1)S(1)} %add_convert_fusion), channel_id=1, source_target_pairs={{0,4},{4,0},{8,12},{12,8},{16,20},{20,16},{24,28},{28,24},{1,5},{5... | collective-permute-start | bytes 1572872 | tf_op jit(solution)/shard_map/ppermute | solution.py:31
  101.3 17.4 %collective-permute-start.10 = (bf16[16,64,256]{2,1,0:T(8,128)(2,1)S(1)}, bf16[16,64,256]{2,1,0:T(8,128)(2,1)S(1)}, u32[]{:S(2)}, u32[]{:S(2)}) collective-permute-start(bf16[16,64,256]{2,1,0:T(8,128)(2,1)S(1)} %collective-permute-done.9), channel_id=1, source_target_pairs={{0,8},{4,12},{8,0},{12,4},{16,24},{20,28},{24,16},{28,20},{1,9},{5... | collective-permute-start | bytes 1572872 | tf_op jit(solution)/shard_map/ppermute | solution.py:31
  105.9 24.0 %collective-permute-start.13 = (bf16[16,64,256]{2,1,0:T(8,128)(2,1)S(1)}, bf16[16,64,256]{2,1,0:T(8,128)(2,1)S(1)}, u32[]{:S(2)}, u32[]{:S(2)}) collective-permute-start(bf16[16,64,256]{2,1,0:T(8,128)(2,1)S(1)} %collective-permute-done.12), channel_id=1, source_target_pairs={{0,8},{4,12},{8,0},{12,4},{16,24},{20,28},{24,16},{28,20},{1,9},{5... | collective-permute-start | bytes 1572872 | tf_op jit(solution)/shard_map/ppermute | solution.py:31
  106.0 34.9 %collective-permute-start.16 = (bf16[16,64,256]{2,1,0:T(8,128)(2,1)S(1)}, bf16[16,64,256]{2,1,0:T(8,128)(2,1)S(1)}, u32[]{:S(2)}, u32[]{:S(2)}) collective-permute-start(bf16[16,64,256]{2,1,0:T(8,128)(2,1)S(1)} %collective-permute-done.15), channel_id=1, source_target_pairs={{0,8},{4,12},{8,0},{12,4},{16,24},{20,28},{24,16},{28,20},{1,9},{5... | collective-permute-start | bytes 1572872 | tf_op jit(solution)/shard_map/ppermute | solution.py:31
  118.7 28.3 %collective-permute-start.11 = (bf16[16,64,256]{2,1,0:T(8,128)(2,1)S(1)}, bf16[16,64,256]{2,1,0:T(8,128)(2,1)S(1)}, u32[]{:S(2)}, u32[]{:S(2)}) collective-permute-start(bf16[16,64,256]{2,1,0:T(8,128)(2,1)S(1)} %collective-permute-done.10), channel_id=1, source_target_pairs={{0,16},{4,20},{8,24},{12,28},{16,0},{20,4},{24,8},{28,12},{1,17},{... | collective-permute-start | bytes 1572872 | tf_op jit(solution)/shard_map/ppermute | solution.py:31
  129.9 17.1 %collective-permute-start.14 = (bf16[16,64,256]{2,1,0:T(8,128)(2,1)S(1)}, bf16[16,64,256]{2,1,0:T(8,128)(2,1)S(1)}, u32[]{:S(2)}, u32[]{:S(2)}) collective-permute-start(bf16[16,64,256]{2,1,0:T(8,128)(2,1)S(1)} %collective-permute-done.13), channel_id=1, source_target_pairs={{0,16},{4,20},{8,24},{12,28},{16,0},{20,4},{24,8},{28,12},{1,17},{... | collective-permute-start | bytes 1572872 | tf_op jit(solution)/shard_map/ppermute | solution.py:31
  140.9 15.4 %collective-permute-start.17 = (bf16[16,64,256]{2,1,0:T(8,128)(2,1)S(1)}, bf16[16,64,256]{2,1,0:T(8,128)(2,1)S(1)}, u32[]{:S(2)}, u32[]{:S(2)}) collective-permute-start(bf16[16,64,256]{2,1,0:T(8,128)(2,1)S(1)} %collective-permute-done.16), channel_id=1, source_target_pairs={{0,16},{4,20},{8,24},{12,28},{16,0},{20,4},{24,8},{28,12},{1,17},{... | collective-permute-start | bytes 1572872 | tf_op jit(solution)/shard_map/ppermute | solution.py:31
where the time goes:
time: 158 us
  starting transfers between devices  65.1 us (41%)
  waiting for transfers between devices  47.8 us (30%)
  matrix products  17 us (11%)
  other arithmetic  15.3 us (10%)
  local copies, waits for them, and re-layouts  11.1 us (7%)
    ppermute x9, waiting for transfers between devices, swapped(): return lax.ppermute(value, axis, pairs)  34.1 us
    ppermute x9, starting transfers between devices, swapped(): return lax.ppermute(value, axis, pairs)  30.5 us
    ppermute x3, starting transfers between devices, shifted(): return lax.ppermute(x, axis, pairs)  19 us
    dot_general x27, matrix products, convolve(): jnp.dot(block, kernel[row_offset], preferred_element_type=jnp.float32)  17 us
    ppermute x3, starting transfers between devices, with_halo(): lax.ppermute(lax.slice_in_dim(block, block.shape[dim] - width, None, axis...  11.3 us
    ppermute x3, waiting for transfers between devices, with_halo(): lax.ppermute(lax.slice_in_dim(block, 0, width, axis=dim), axis, backward)  8.64 us
    slice x9, local copies, waits for them, and re-layouts, convolve(): columns[row_offset:row_offset + rows_out]  5.69 us
    select_n x3, other arithmetic, on_device(): section_in = jnp.where(decoder_enabled, joined, incoming)  4.54 us
  transfers between devices with their start and end apart: 18, of which 11 were waited for; matrix products, arithmetic and copies ran while one was open for 9% of the time, Pallas kernels for 0%

commit v1 on v0

v1 whole, which is shorter than its diff:
```python
import functools

import jax
import jax.numpy as jnp
from jax import lax
from jax.experimental import pallas as pl
from jax.experimental.pallas import tpu as pltpu
from jax.sharding import PartitionSpec as P

BF16 = jnp.bfloat16
F32 = jnp.float32


def split(total, most):
    parts = -(-total // most)
    sizes = [total // parts + (1 if i < total % parts else 0) for i in range(parts)]
    out, at = [], 0
    for size in sizes:
        out.append((at, size))
        at += size
    return out


def body(
    ticks, rows, w, c,
    held, skips_in, arrivals, kern, bias,
    maps, stash,
    inc, sk, sec, halo, kv, x0, x1, x2, outb,
    inc_rs, shift_ss, halo_ss, halo_rs, st_ss, st_rs, fwd_ss, out_s, k_s, sk_s,
):
    n = lax.axis_size("segment")
    nz = lax.axis_size("rows")
    s = lax.axis_index("segment")
    z = lax.axis_index("rows")
    half = n // 2
    last = ticks - 1
    encoder = s < half
    decoder = s >= half
    middle = s == half
    has_next = s < n - 1
    has_prev = s >= 1
    has_up = z >= 1
    has_down = z < nz - 1
    relayed = encoder & (s % 2 == 1) & (s < half - 1)
    relays = encoder & (s % 2 == 0) & (s >= 2)
    from_relay = (s > half) & (s % 2 == 0)
    direct = encoder & (s % 2 == 0) & (s < half - 1)
    mirror = n - 1 - s
    q = rows // 4
    pieces = ((0, q), (rows - q, q), (q, rows - 2 * q))

    def at(segment, row):
        return {"segment": segment, "rows": row}

    barrier = pltpu.get_barrier_semaphore()
    links = (
        (has_next, s + 1, z),
        (has_prev, s - 1, z),
        (encoder | decoder, mirror, z),
        (relays | from_relay, n - s, z),
        (has_up, s, z - 1),
        (has_down, s, z + 1),
    )
    partners = 0
    for cond, seg, row in links:
        @pl.when(cond)
        def _():
            pl.semaphore_signal(barrier, inc=1, device_id=at(seg, row), device_id_type=pl.DeviceIdType.MESH)
        partners = partners + cond.astype(jnp.int32)

    k_copies = [pltpu.make_async_copy(kern.at[l], kv.at[l], k_s.at[l]) for l in range(3)]
    for copy in k_copies:
        copy.start()
    skip_copy = pltpu.make_async_copy(skips_in, sk, sk_s.at[0])

    @pl.when(decoder)
    def _():
        skip_copy.start()

    @pl.when(s == 0)
    def _():
        for t in range(ticks):
            for p, (r, m) in enumerate(pieces):
                pltpu.make_async_copy(
                    arrivals.at[t, pl.ds(r * w, m * w)], inc.at[t, pl.ds(r * w, m * w)], inc_rs.at[t, p]
                ).start()

    pl.semaphore_wait(barrier, partners)

    def remote(src, dst, ss, rs, seg, row):
        return pltpu.make_async_remote_copy(
            src_ref=src, dst_ref=dst, send_sem=ss, recv_sem=rs, device_id=at(seg, row),
            device_id_type=pl.DeviceIdType.MESH,
        )

    def shift_copy(src, t, p):
        r, m = pieces[p]
        rng = pl.ds(r * w, m * w)
        return remote(src.at[rng], inc.at[t, rng], shift_ss.at[t, p], inc_rs.at[t, p], s + 1, z)

    def stash_copy(t, p):
        r, m = pieces[p]
        rng = pl.ds(r * w, m * w)
        return remote(outb.at[t, rng], stash.at[t, rng], st_ss.at[t, p], st_rs.at[t, p], mirror, z)

    def relay_copy(t, p):
        r, m = pieces[p]
        rng = pl.ds(r * w, m * w)
        return remote(inc.at[t + 1, rng], stash.at[t, rng], fwd_ss.at[t, p], st_rs.at[t, p], n - s, z)

    def keep_copy(t, p):
        r, m = pieces[p]
        rng = pl.ds(r * w, m * w)
        return pltpu.make_async_copy(inc.at[t + 1, rng], stash.at[t, rng], st_rs.at[t, p])

    @pl.when(has_next)
    def _():
        for p in range(3):
            shift_copy(held, 0, p).start()

    e = 3 * w

    def up_copy(t):
        return remote(sec.at[t, 0], halo.at[t, 1], halo_ss.at[t, 0], halo_rs.at[t, 1], s, z - 1)

    def down_copy(t):
        return remote(sec.at[t, 1], halo.at[t, 0], halo_ss.at[t, 1], halo_rs.at[t, 0], s, z + 1)

    @pl.when(encoder)
    def _():
        sk[...] = jnp.zeros_like(sk)

    @pl.when(jnp.logical_not(has_up))
    def _():
        for t in range(ticks):
            halo[t, 0] = jnp.zeros((e, c), BF16)

    @pl.when(jnp.logical_not(has_down))
    def _():
        for t in range(ticks):
            halo[t, 1] = jnp.zeros((e, c), BF16)

    def put(dst, row, a):
        m = a.shape[0]
        col = lax.rem(lax.broadcasted_iota(jnp.int32, a.shape, 0), w)
        rng = pl.ds(row * w, m)
        dst[rng, c : 2 * c] = a.astype(BF16)
        dst[rng, 0:c] = jnp.where(col == 0, 0.0, pltpu.roll(a, 1, 0)).astype(BF16)
        dst[rng, 2 * c : 3 * c] = jnp.where(col == w - 1, 0.0, pltpu.roll(a, m - 1, 0)).astype(BF16)

    def patches(src, base, count):
        return jnp.concatenate([src[pl.ds((base + d) * w, count * w), :] for d in range(3)], axis=1)

    def conv(lhs, l):
        return jnp.dot(lhs, kv[l], preferred_element_type=F32) + bias[pl.ds(l, 1), :]

    def silu(v):
        return v / (1.0 + jnp.exp(-v))

    up_i = has_up.astype(jnp.int32)
    down_i = has_down.astype(jnp.int32)

    for t in range(ticks):
        mid_t = middle if t >= 1 else None

        def joined(r, m):
            rng = pl.ds(r * w, m * w)
            x = inc[t, rng].astype(F32)
            add = sk[t, rng].astype(F32)
            if mid_t is not None:
                add = jnp.where(mid_t, x, add)
            return (x + add).astype(BF16)

        def arrived(p):
            r, m = pieces[p]
            view = inc.at[t, pl.ds(r * w, m * w)]
            pltpu.make_async_copy(view, view, inc_rs.at[t, p]).wait()
            if t >= 1:
                @pl.when(relays)
                def _():
                    relay_copy(t - 1, p).start()

                @pl.when(middle)
                def _():
                    keep_copy(t - 1, p).start()

        if t == 0:
            @pl.when(decoder)
            def _():
                skip_copy.wait()

        arrived(0)
        top = joined(0, q)
        sec[t, 0] = top[0:e]

        @pl.when(has_up)
        def _():
            up_copy(t).start()

        put(x0, 3, top.astype(F32))
        arrived(1)
        bottom = joined(rows - q, q)
        sec[t, 1] = bottom[q * w - e :]

        @pl.when(has_down)
        def _():
            down_copy(t).start()

        put(x0, 3 + rows - q, bottom.astype(F32))
        arrived(2)
        for r, m in split(rows - 2 * q, 4):
            put(x0, 3 + q + r, joined(q + r, m).astype(F32))
        if t == 0:
            k_copies[0].wait()
        for r, m in split(rows - 2, 7):
            put(x1, 3 + r, silu(conv(patches(x0, 3 + r, m), 0)))

        @pl.when(has_down)
        def _():
            remote(sec.at[t, 0], halo.at[t, 1], halo_ss.at[t, 0], halo_rs.at[t, 1], s, z).wait_recv()

        @pl.when(has_up)
        def _():
            remote(sec.at[t, 1], halo.at[t, 0], halo_ss.at[t, 1], halo_rs.at[t, 0], s, z).wait_recv()

        put(x0, 0, halo[t, 0].astype(F32))
        put(x0, 3 + rows, halo[t, 1].astype(F32))
        edge = silu(conv(jnp.concatenate([patches(x0, 0, 3), patches(x0, rows + 1, 3)], axis=0), 0))
        idx = lax.broadcasted_iota(jnp.int32, edge.shape, 0)
        inside = jnp.where(idx < 2 * w, up_i, jnp.where(idx >= 4 * w, down_i, 1)) > 0
        edge = jnp.where(inside, edge, 0.0)
        put(x1, 0, edge[0:e])
        put(x1, rows + 1, edge[e:])

        if t == 0:
            k_copies[1].wait()
        for r, m in split(rows + 2, 6):
            a = silu(conv(patches(x1, r, m), 1))
            if r == 0 or r + m == rows + 2:
                idx = lax.broadcasted_iota(jnp.int32, a.shape, 0)
                inside = jnp.where(idx < w, up_i, 1) if r == 0 else jnp.where(idx >= (m - 1) * w, down_i, 1)
                a = jnp.where(inside > 0, a, 0.0)
            put(x2, r, a)

        if t == 0:
            k_copies[2].wait()

        def emit(p):
            if t < last:
                @pl.when(has_next)
                def _():
                    shift_copy(outb.at[t], t + 1, p).start()

                @pl.when(direct)
                def _():
                    stash_copy(t, p).start()
            else:
                @pl.when(encoder)
                def _():
                    stash_copy(t, p).start()

        def own(r, m):
            return x0[pl.ds((3 + r) * w, m * w), c : 2 * c].astype(F32)

        ends = conv(jnp.concatenate([patches(x2, 0, q), patches(x2, rows - q, q)], axis=0), 2)
        outb[t, 0 : q * w] = (own(0, q) + ends[0 : q * w]).astype(BF16)
        emit(0)
        outb[t, (rows - q) * w :] = (own(rows - q, q) + ends[q * w :]).astype(BF16)
        emit(1)
        for r, m in split(rows - 2 * q, 8):
            outb[t, pl.ds((q + r) * w, m * w)] = (own(q + r, m) + conv(patches(x2, q + r, m), 2)).astype(BF16)
        emit(2)
        pltpu.make_async_copy(outb.at[t], maps.at[t], out_s.at[t]).start()

    for t in range(ticks):
        @pl.when(has_up)
        def _():
            up_copy(t).wait_send()

        @pl.when(has_down)
        def _():
            down_copy(t).wait_send()

        for p in range(3):
            @pl.when(has_next)
            def _():
                shift_copy(held if t == 0 else outb.at[t - 1], t, p).wait_send()

            if t < last:
                @pl.when(relays)
                def _():
                    relay_copy(t, p).wait_send()

                @pl.when(direct)
                def _():
                    stash_copy(t, p).wait_send()

                @pl.when(decoder)
                def _():
                    keep_copy(t, p).wait()
            else:
                @pl.when(encoder)
                def _():
                    stash_copy(t, p).wait_send()

                @pl.when(decoder)
                def _():
                    stash_copy(t, p).wait_recv()
        pltpu.make_async_copy(outb.at[t], maps.at[t], out_s.at[t]).wait()


def on_device(held_maps, held_skips, arrivals, kernels, biases):
    ticks, _, rows, w, c = held_skips.shape
    flat = rows * w
    any_spec = pl.BlockSpec(memory_space=pl.ANY)
    shape = jax.ShapeDtypeStruct((ticks, flat, c), BF16)
    dma = pltpu.SemaphoreType.DMA
    maps, stash = pl.pallas_call(
        functools.partial(body, ticks, rows, w, c),
        out_shape=(shape, shape),
        in_specs=[any_spec] * 4 + [pl.BlockSpec(memory_space=pltpu.VMEM)],
        out_specs=(any_spec, any_spec),
        scratch_shapes=[
            pltpu.VMEM((ticks, flat, c), BF16),
            pltpu.VMEM((ticks, flat, c), BF16),
            pltpu.VMEM((ticks, 2, 3 * w, c), BF16),
            pltpu.VMEM((ticks, 2, 3 * w, c), BF16),
            pltpu.VMEM((3, 9 * c, c), BF16),
            pltpu.VMEM(((rows + 6) * w, 3 * c), BF16),
            pltpu.VMEM(((rows + 4) * w, 3 * c), BF16),
            pltpu.VMEM(((rows + 2) * w, 3 * c), BF16),
            pltpu.VMEM((ticks, flat, c), BF16),
            dma((ticks, 3)),
            dma((ticks, 3)),
            dma((ticks, 2)),
            dma((ticks, 2)),
            dma((ticks, 3)),
            dma((ticks, 3)),
            dma((ticks, 3)),
            dma((ticks,)),
            dma((3,)),
            dma((1,)),
        ],
        compiler_params=pltpu.CompilerParams(
            collective_id=0, has_side_effects=True, vmem_limit_bytes=48 * 1024 * 1024
        ),
    )(
        held_maps.reshape(flat, c),
        held_skips.reshape(ticks, flat, c),
        arrivals.reshape(ticks, flat, c),
        kernels.reshape(3, 9 * c, c),
        biases[0],
    )
    decoder = lax.axis_index("segment") >= lax.axis_size("segment") // 2
    stash = jnp.where(decoder, stash, jnp.zeros_like(stash))
    full = (ticks, 1, rows, w, c)
    return maps.reshape(full), stash.reshape(full)


def solution(mesh):
    placed = (
        P("segment", "rows", None, None),
        P(None, "segment", "rows", None, None),
        P(None, "rows", None, None),
        P("segment", None, None, None, None),
        P("segment", None, None),
    )
    return jax.shard_map(
        on_device,
        mesh=mesh,
        in_specs=placed,
        out_specs=(P(None, "segment", "rows", None, None), P(None, "segment", "rows", None, None)),
        check_vma=False,
    )
```

time: 158 us -> 60.3 us (0.38)
  the two profiles are of different devices: /device:TPU:0 before, /device:TPU:13 now
where the time goes in v1:
time: 60.3 us; the launch traced here: 60.1 us
  Pallas kernels  53.9 us (89%)
  local copies, waits for them, and re-layouts  4.28 us (7%)
  other arithmetic  1.25 us (2%)
  between operations  0.65 us (1%)
    pallas_call x1, Pallas kernels, on_device(): pl.pallas_call(functools.partial(body, ticks, rows, w, c), out_shape=(sha...  53.9 us
    unnamed x6, local copies, waits for them, and re-layouts  4.28 us
    select_n x1, other arithmetic, on_device(): stash = jnp.where(decoder, stash, jnp.zeros_like(stash))  1.25 us

profile of v1, /device:TPU:13, one launch (start us, length us, event | category | flops | bytes accessed | tf_op | source)
XLA Modules:
  0.0 60.1 jit_solution(1533194838485934217)
XLA Ops:
  0.6 0.7 %copy.11 = f32[1,3,256]{2,1,0:T(4,128)S(1)} copy(f32[1,3,256]{2,0,1:T(1,128)} %param.9) | data formatting | bytes 6144
  1.3 0.0 copy-start
  1.3 1.4 %copy-done = bf16[3,1,16,64,256]{4,3,2,1,0:T(8,128)(2,1)S(1)} copy-done((bf16[3,1,16,64,256]{4,3,2,1,0:T(8,128)(2,1)S(1)}, bf16[3,1,16,64,256]{4,3,2,1,0:T(8,128)(2,1)}, u32[]{:S(2)}) %copy-start) | copy-done | bytes 1572888
  2.7 0.0 copy-start.1
  2.7 1.0 %copy-done.1 = bf16[1,16,64,256]{3,2,1,0:T(8,128)(2,1)S(1)} copy-done((bf16[1,16,64,256]{3,2,1,0:T(8,128)(2,1)S(1)}, bf16[1,16,64,256]{3,2,1,0:T(8,128)(2,1)}, u32[]{:S(2)}) %copy-start.1) | copy-done | bytes 524312
  3.8 53.9 %shard_map.68 = (bf16[3,1024,256]{2,1,0:T(8,128)(2,1)S(1)}, bf16[3,1024,256]{2,1,0:T(8,128)(2,1)S(1)}) custom-call(bf16[1024,256]{1,0:T(8,128)(2,1)S(1)} %bitcast.15, bf16[3,1024,256]{2,1,0:T(8,128)(2,1)S(1)} %bitcast.14, bf16[3,1024,256]{2,1,0:T(8,128)(2,1)} %bitcast.18, bf16[3,2304,256]{2,1,0:T(8,128)(2,1)} %bitcast.17, f32[3,256]{1,0:T(4,128)S(1)} %bitcast.16), custom_call_target="tpu_custom_call" | custom-call | tf_op jit(solution)/shard_map/pallas_call | solution.py:318
  57.7 1.3 %broadcast_select_fusion = bf16[3,1024,256]{2,1,0:T(8,128)(2,1)} fusion(bf16[3,1024,256]{2,1,0:T(8,128)(2,1)S(1)} %get-tuple-element.5, pred[]{:T(512)S(6)} %ge.3), kind=kLoop, calls=%fused_computation | loop fusion | flops 786432 | bytes 3145729 | tf_op jit(solution)/shard_map/jit(_where)/select_n | solution.py:355
  58.9 1.1 %copy.13 = bf16[3,1,16,64,256]{4,3,2,1,0:T(8,128)(2,1)} copy(bf16[3,1,16,64,256]{4,3,2,1,0:T(8,128)(2,1)S(1)} %bitcast.13) | data formatting | bytes 3145728
Async XLA Ops:
  1.3 1.4 %copy-start = (bf16[3,1,16,64,256]{4,3,2,1,0:T(8,128)(2,1)S(1)}, bf16[3,1,16,64,256]{4,3,2,1,0:T(8,128)(2,1)}, u32[]{:S(2)}) copy-start(bf16[3,1,16,64,256]{4,3,2,1,0:T(8,128)(2,1)} %param.6) | copy-start | bytes 4718596
  2.7 1.0 %copy-start.1 = (bf16[1,16,64,256]{3,2,1,0:T(8,128)(2,1)S(1)}, bf16[1,16,64,256]{3,2,1,0:T(8,128)(2,1)}, u32[]{:S(2)}) copy-start(bf16[1,16,64,256]{3,2,1,0:T(8,128)(2,1)} %param.5) | copy-start | bytes 1572868

commit v2 on v1

--- a/solution.py
+++ b/solution.py
@@ -11,22 +11,12 @@
 F32 = jnp.float32
 
 
-def split(total, most):
-    parts = -(-total // most)
-    sizes = [total // parts + (1 if i < total % parts else 0) for i in range(parts)]
-    out, at = [], 0
-    for size in sizes:
-        out.append((at, size))
-        at += size
-    return out
-
-
 def body(
     ticks, rows, w, c,
-    held, skips_in, arrivals, kern, bias,
+    held, skips_in, arrivals, kern, bias_in,
     maps, stash,
-    inc, sk, sec, halo, kv, x0, x1, x2, outb,
-    inc_rs, shift_ss, halo_ss, halo_rs, st_ss, st_rs, fwd_ss, out_s, k_s, sk_s,
+    inc, sk, sec, halo, kv, bias, x0, x1, x2, outb,
+    inc_rs, shift_ss, halo_ss, halo_rs, st_ss, st_rs, fwd_ss, out_s, k_s, sk_s, b_s,
 ):
     n = lax.axis_size("segment")
     nz = lax.axis_size("rows")
@@ -46,8 +36,10 @@
     from_relay = (s > half) & (s % 2 == 0)
     direct = encoder & (s % 2 == 0) & (s < half - 1)
     mirror = n - 1 - s
-    q = rows // 4
-    pieces = ((0, q), (rows - q, q), (q, rows - 2 * q))
+    q = 3
+    h = (rows - 2 * q + 1) // 2
+    pieces = ((0, q), (rows - q, q), (q, h), (q + h, rows - 2 * q - h))
+    count = len(pieces)
 
     def at(segment, row):
         return {"segment": segment, "rows": row}
@@ -71,6 +63,8 @@
     k_copies = [pltpu.make_async_copy(kern.at[l], kv.at[l], k_s.at[l]) for l in range(3)]
     for copy in k_copies:
         copy.start()
+    bias_copy = pltpu.make_async_copy(bias_in, bias, b_s.at[0])
+    bias_copy.start()
     skip_copy = pltpu.make_async_copy(skips_in, sk, sk_s.at[0])
 
     @pl.when(decoder)
@@ -115,7 +109,7 @@
 
     @pl.when(has_next)
     def _():
-        for p in range(3):
+        for p in range(count):
             shift_copy(held, 0, p).start()
 
     e = 3 * w
@@ -142,28 +136,57 @@
 
     def put(dst, row, a):
         m = a.shape[0]
-        col = lax.rem(lax.broadcasted_iota(jnp.int32, a.shape, 0), w)
         rng = pl.ds(row * w, m)
         dst[rng, c : 2 * c] = a.astype(BF16)
-        dst[rng, 0:c] = jnp.where(col == 0, 0.0, pltpu.roll(a, 1, 0)).astype(BF16)
-        dst[rng, 2 * c : 3 * c] = jnp.where(col == w - 1, 0.0, pltpu.roll(a, m - 1, 0)).astype(BF16)
-
-    def patches(src, base, count):
-        return jnp.concatenate([src[pl.ds((base + d) * w, count * w), :] for d in range(3)], axis=1)
-
-    def conv(lhs, l):
-        return jnp.dot(lhs, kv[l], preferred_element_type=F32) + bias[pl.ds(l, 1), :]
+        sub = lax.broadcasted_iota(jnp.int32, (m // w, 8, c), 1)
+        left = pltpu.roll(a, 1, 0).reshape(m // w, w, c)
+        first = jnp.where(sub == 0, 0.0, left[:, 0:8])
+        dst[rng, 0:c] = jnp.concatenate([first, left[:, 8:]], axis=1).reshape(m, c).astype(BF16)
+        right = pltpu.roll(a, m - 1, 0).reshape(m // w, w, c)
+        final = jnp.where(sub == 7, 0.0, right[:, w - 8 :])
+        dst[rng, 2 * c : 3 * c] = jnp.concatenate([right[:, 0 : w - 8], final], axis=1).reshape(m, c).astype(BF16)
+
+    def patches(src, spans):
+        return jnp.concatenate(
+            [jnp.concatenate([src[pl.ds((b + d) * w, m * w), :] for b, m in spans], axis=0) for d in range(3)], axis=1
+        )
 
     def silu(v):
-        return v / (1.0 + jnp.exp(-v))
+        return v * (0.5 + 0.5 * jnp.tanh(0.5 * v))
 
     up_i = has_up.astype(jnp.int32)
     down_i = has_down.astype(jnp.int32)
+    pending = []
+
+    def flush():
+        while pending:
+            pending.pop(0)()
+
+    def step(src, spans, l, finish):
+        acc = jnp.dot(patches(src, spans), kv[l], preferred_element_type=F32)
+        flush()
+        pending.append(lambda: finish(acc + bias[l]))
+
+    def store(dst, shift, spans, guard=0):
+        def finish(v):
+            v = silu(v)
+            if guard:
+                idx = lax.broadcasted_iota(jnp.int32, v.shape, 0)
+                low = jnp.where(idx < guard * w, up_i, 1)
+                inside = jnp.where(idx >= v.shape[0] - guard * w, down_i, low)
+                v = jnp.where(inside > 0, v, 0.0)
+            at_row = 0
+            for b, m in spans:
+                put(dst, b + shift, v[at_row * w : (at_row + m) * w])
+                at_row += m
+
+        return finish
 
     for t in range(ticks):
         mid_t = middle if t >= 1 else None
 
-        def joined(r, m):
+        def joined(p):
+            r, m = pieces[p]
             rng = pl.ds(r * w, m * w)
             x = inc[t, rng].astype(F32)
             add = sk[t, rng].astype(F32)
@@ -184,36 +207,70 @@
                 def _():
                     keep_copy(t - 1, p).start()
 
+        def emit(p):
+            if t < last:
+                @pl.when(has_next)
+                def _():
+                    shift_copy(outb.at[t], t + 1, p).start()
+
+                @pl.when(direct)
+                def _():
+                    stash_copy(t, p).start()
+            else:
+                @pl.when(encoder)
+                def _():
+                    stash_copy(t, p).start()
+
+        def result(spans, ps):
+            def finish(v):
+                at_row = 0
+                for b, m in spans:
+                    own = x0[pl.ds((3 + b) * w, m * w), c : 2 * c].astype(F32)
+                    outb[t, pl.ds(b * w, m * w)] = (own + v[at_row * w : (at_row + m) * w]).astype(BF16)
+                    at_row += m
+                for p in ps:
+                    emit(p)
+
+            return finish
+
+        def spans_at(spans, base):
+            return tuple((b + base, m) for b, m in spans)
+
         if t == 0:
             @pl.when(decoder)
             def _():
                 skip_copy.wait()
 
         arrived(0)
-        top = joined(0, q)
-        sec[t, 0] = top[0:e]
+        top = joined(0)
+        sec[t, 0] = top
 
         @pl.when(has_up)
         def _():
             up_copy(t).start()
 
+        arrived(1)
+        bottom = joined(1)
+        sec[t, 1] = bottom
+
+        @pl.when(has_down)
+        def _():
+            down_copy(t).start()
+
         put(x0, 3, top.astype(F32))
-        arrived(1)
-        bottom = joined(rows - q, q)
-        sec[t, 1] = bottom[q * w - e :]
-
-        @pl.when(has_down)
-        def _():
-            down_copy(t).start()
-
         put(x0, 3 + rows - q, bottom.astype(F32))
         arrived(2)
-        for r, m in split(rows - 2 * q, 4):
-            put(x0, 3 + q + r, joined(q + r, m).astype(F32))
+        put(x0, 3 + pieces[2][0], joined(2).astype(F32))
         if t == 0:
+            bias_copy.wait()
             k_copies[0].wait()
-        for r, m in split(rows - 2, 7):
-            put(x1, 3 + r, silu(conv(patches(x0, 3 + r, m), 0)))
+        a_end = q + h - 2
+        first = ((1, a_end),)
+        second = ((1 + a_end, rows - 2 - a_end),)
+        step(x0, spans_at(first, 2), 0, store(x1, 2, first))
+        arrived(3)
+        put(x0, 3 + pieces[3][0], joined(3).astype(F32))
+        step(x0, spans_at(second, 2), 0, store(x1, 2, second))
 
         @pl.when(has_down)
         def _():
@@ -225,51 +282,23 @@
 
         put(x0, 0, halo[t, 0].astype(F32))
         put(x0, 3 + rows, halo[t, 1].astype(F32))
-        edge = silu(conv(jnp.concatenate([patches(x0, 0, 3), patches(x0, rows + 1, 3)], axis=0), 0))
-        idx = lax.broadcasted_iota(jnp.int32, edge.shape, 0)
-        inside = jnp.where(idx < 2 * w, up_i, jnp.where(idx >= 4 * w, down_i, 1)) > 0
-        edge = jnp.where(inside, edge, 0.0)
-        put(x1, 0, edge[0:e])
-        put(x1, rows + 1, edge[e:])
-
+        edge1 = ((-2, 3), (rows - 1, 3))
+        step(x0, spans_at(edge1, 2), 0, store(x1, 2, edge1, 2))
         if t == 0:
             k_copies[1].wait()
-        for r, m in split(rows + 2, 6):
-            a = silu(conv(patches(x1, r, m), 1))
-            if r == 0 or r + m == rows + 2:
-                idx = lax.broadcasted_iota(jnp.int32, a.shape, 0)
-                inside = jnp.where(idx < w, up_i, 1) if r == 0 else jnp.where(idx >= (m - 1) * w, down_i, 1)
-                a = jnp.where(inside > 0, a, 0.0)
-            put(x2, r, a)
-
+        ring2 = ((2, 3), (rows - 5, 3))
+        step(x1, spans_at(ring2, 1), 1, store(x2, 1, ring2))
+        edge2 = ((-1, 3), (rows - 2, 3))
+        step(x1, spans_at(edge2, 1), 1, store(x2, 1, edge2, 1))
+        core2 = ((5, rows - 10),)
+        step(x1, spans_at(core2, 1), 1, store(x2, 1, core2))
         if t == 0:
             k_copies[2].wait()
-
-        def emit(p):
-            if t < last:
-                @pl.when(has_next)
-                def _():
-                    shift_copy(outb.at[t], t + 1, p).start()
-
-                @pl.when(direct)
-                def _():
-                    stash_copy(t, p).start()
-            else:
-                @pl.when(encoder)
-                def _():
-                    stash_copy(t, p).start()
-
-        def own(r, m):
-            return x0[pl.ds((3 + r) * w, m * w), c : 2 * c].astype(F32)
-
-        ends = conv(jnp.concatenate([patches(x2, 0, q), patches(x2, rows - q, q)], axis=0), 2)
-        outb[t, 0 : q * w] = (own(0, q) + ends[0 : q * w]).astype(BF16)
-        emit(0)
-        outb[t, (rows - q) * w :] = (own(rows - q, q) + ends[q * w :]).astype(BF16)
-        emit(1)
-        for r, m in split(rows - 2 * q, 8):
-            outb[t, pl.ds((q + r) * w, m * w)] = (own(q + r, m) + conv(patches(x2, q + r, m), 2)).astype(BF16)
-        emit(2)
+        ends = (pieces[0], pieces[1])
+        step(x2, ends, 2, result(ends, (0, 1)))
+        for p in (2, 3):
+            step(x2, (pieces[p],), 2, result((pieces[p],), (p,)))
+        flush()
         pltpu.make_async_copy(outb.at[t], maps.at[t], out_s.at[t]).start()
 
     for t in range(ticks):
@@ -281,7 +310,7 @@
         def _():
             down_copy(t).wait_send()
 
-        for p in range(3):
+        for p in range(count):
             @pl.when(has_next)
             def _():
                 shift_copy(held if t == 0 else outb.at[t - 1], t, p).wait_send()
@@ -318,7 +347,7 @@
     maps, stash = pl.pallas_call(
         functools.partial(body, ticks, rows, w, c),
         out_shape=(shape, shape),
-        in_specs=[any_spec] * 4 + [pl.BlockSpec(memory_space=pltpu.VMEM)],
+        in_specs=[any_spec] * 5,
         out_specs=(any_spec, any_spec),
         scratch_shapes=[
             pltpu.VMEM((ticks, flat, c), BF16),
@@ -326,30 +355,32 @@
             pltpu.VMEM((ticks, 2, 3 * w, c), BF16),
             pltpu.VMEM((ticks, 2, 3 * w, c), BF16),
             pltpu.VMEM((3, 9 * c, c), BF16),
+            pltpu.VMEM((3, 1, c), F32),
             pltpu.VMEM(((rows + 6) * w, 3 * c), BF16),
             pltpu.VMEM(((rows + 4) * w, 3 * c), BF16),
             pltpu.VMEM(((rows + 2) * w, 3 * c), BF16),
             pltpu.VMEM((ticks, flat, c), BF16),
-            dma((ticks, 3)),
-            dma((ticks, 3)),
+            dma((ticks, 4)),
+            dma((ticks, 4)),
             dma((ticks, 2)),
             dma((ticks, 2)),
-            dma((ticks, 3)),
-            dma((ticks, 3)),
-            dma((ticks, 3)),
+            dma((ticks, 4)),
+            dma((ticks, 4)),
+            dma((ticks, 4)),
             dma((ticks,)),
             dma((3,)),
             dma((1,)),
+            dma((1,)),
         ],
         compiler_params=pltpu.CompilerParams(
-            collective_id=0, has_side_effects=True, vmem_limit_bytes=48 * 1024 * 1024
+            collective_id=0, has_side_effects=True, vmem_limit_bytes=63 * 1024 * 1024
         ),
     )(
         held_maps.reshape(flat, c),
         held_skips.reshape(ticks, flat, c),
         arrivals.reshape(ticks, flat, c),
         kernels.reshape(3, 9 * c, c),
-        biases[0],
+        biases.reshape(3, 1, c),
     )
     decoder = lax.axis_index("segment") >= lax.axis_size("segment") // 2
     stash = jnp.where(decoder, stash, jnp.zeros_like(stash))

time: 60.3 us -> 58 us (0.962)
  local copies, waits for them, and re-layouts: 4.28 us -> 1.15 us
  other arithmetic: 1.25 us -> 2.78 us
  Pallas kernels: 53.9 us -> 53.2 us
    unnamed x6 -> x3, local copies, waits for them, and re-layouts: 4.28 us -> 1.15 us
    select_n x1, other arithmetic: 1.25 us -> 2.78 us  [on_device(): stash = jnp.where(decoder, stash, jnp.zeros_like(stash))]
    pallas_call x1, Pallas kernels: 53.9 us -> 53.2 us  [on_device(): pl.pallas_call(functools.partial(body, ticks, rows, w, c), out_shape=(sha...]
where the time goes in v2:
time: 58 us; the launch traced here: 57.8 us
  Pallas kernels  53.2 us (92%)
  other arithmetic  2.78 us (5%)
  local copies, waits for them, and re-layouts  1.15 us (2%)
  between operations  0.65 us (1%)
    pallas_call x1, Pallas kernels, on_device(): pl.pallas_call(functools.partial(body, ticks, rows, w, c), out_shape=(sha...  53.2 us
    select_n x1, other arithmetic, on_device(): stash = jnp.where(decoder, stash, jnp.zeros_like(stash))  2.78 us

profile of v2, /device:TPU:13, one launch (start us, length us, event | category | flops | bytes accessed | tf_op | source)
XLA Modules:
  0.0 57.8 jit_solution(18434133907598686132)
XLA Ops:
  0.6 53.2 %shard_map.68 = (bf16[3,1024,256]{2,1,0:T(8,128)(2,1)}, bf16[3,1024,256]{2,1,0:T(8,128)(2,1)}) custom-call(bf16[1024,256]{1,0:T(8,128)(2,1)} %bitcast.16, bf16[3,1024,256]{2,1,0:T(8,128)(2,1)} %bitcast.13, bf16[3,1024,256]{2,1,0:T(8,128)(2,1)} %bitcast.14, bf16[3,2304,256]{2,1,0:T(8,128)(2,1)} %bitcast.11, f32[3,1,256]{2,1,0:T(1,128)} %bitcast.17), custom_call_target="tpu_custom_call" | custom-call | tf_op jit(solution)/shard_map/pallas_call | solution.py:347
  53.9 0.0 copy-start
  53.9 2.8 %broadcast_select_fusion = bf16[3,1024,256]{2,1,0:T(8,128)(2,1)} fusion(bf16[3,1024,256]{2,1,0:T(8,128)(2,1)} %get-tuple-element.5, pred[]{:T(512)S(6)} %ge.3), kind=kLoop, calls=%fused_computation | loop fusion | flops 786432 | bytes 3145729 | tf_op jit(solution)/shard_map/jit(_where)/select_n | solution.py:386
  56.7 0.0 copy-done
  56.7 1.1 %copy.10 = bf16[3,1,16,64,256]{4,3,2,1,0:T(8,128)(2,1)} copy(bf16[3,1,16,64,256]{4,3,2,1,0:T(8,128)(2,1)S(1)} %bitcast.12) | data formatting | bytes 3145728
Async XLA Ops:
  53.9 2.8 %copy-start = (bf16[3,1024,256]{2,1,0:T(8,128)(2,1)S(1)}, bf16[3,1024,256]{2,1,0:T(8,128)(2,1)}, u32[]{:S(2)}) copy-start(bf16[3,1024,256]{2,1,0:T(8,128)(2,1)} %get-tuple-element.4) | copy-start | bytes 4718596

commit v3 on v2

--- a/solution.py
+++ b/solution.py
@@ -146,11 +146,6 @@
         final = jnp.where(sub == 7, 0.0, right[:, w - 8 :])
         dst[rng, 2 * c : 3 * c] = jnp.concatenate([right[:, 0 : w - 8], final], axis=1).reshape(m, c).astype(BF16)
 
-    def patches(src, spans):
-        return jnp.concatenate(
-            [jnp.concatenate([src[pl.ds((b + d) * w, m * w), :] for b, m in spans], axis=0) for d in range(3)], axis=1
-        )
-
     def silu(v):
         return v * (0.5 + 0.5 * jnp.tanh(0.5 * v))
 
@@ -162,23 +157,23 @@
         while pending:
             pending.pop(0)()
 
-    def step(src, spans, l, finish):
-        acc = jnp.dot(patches(src, spans), kv[l], preferred_element_type=F32)
-        flush()
-        pending.append(lambda: finish(acc + bias[l]))
-
-    def store(dst, shift, spans, guard=0):
-        def finish(v):
-            v = silu(v)
-            if guard:
+    def step(src, base, spans, l, finish):
+        for b, m in spans:
+            for o in range(0, m, 3):
+                k = min(3, m - o)
+                acc = sum(jnp.dot(src[pl.ds((base + b + o + d) * w, k * w), :], kv[l, pl.ds(3 * c * d, 3 * c), :], preferred_element_type=F32) for d in range(3))
+                flush()
+                pending.append(functools.partial(finish, b + o, k, acc))
+
+    def store(dst, shift, l):
+        def finish(b, m, acc):
+            v = silu(acc + bias[l])
+            low, high = max(0, -b), max(0, b + m - rows)
+            if low or high:
                 idx = lax.broadcasted_iota(jnp.int32, v.shape, 0)
-                low = jnp.where(idx < guard * w, up_i, 1)
-                inside = jnp.where(idx >= v.shape[0] - guard * w, down_i, low)
+                inside = jnp.where(idx < low * w, up_i, jnp.where(idx >= (m - high) * w, down_i, 1))
                 v = jnp.where(inside > 0, v, 0.0)
-            at_row = 0
-            for b, m in spans:
-                put(dst, b + shift, v[at_row * w : (at_row + m) * w])
-                at_row += m
+            put(dst, b + shift, v)
 
         return finish
 
@@ -221,20 +216,9 @@
                 def _():
                     stash_copy(t, p).start()
 
-        def result(spans, ps):
-            def finish(v):
-                at_row = 0
-                for b, m in spans:
-                    own = x0[pl.ds((3 + b) * w, m * w), c : 2 * c].astype(F32)
-                    outb[t, pl.ds(b * w, m * w)] = (own + v[at_row * w : (at_row + m) * w]).astype(BF16)
-                    at_row += m
-                for p in ps:
-                    emit(p)
-
-            return finish
-
-        def spans_at(spans, base):
-            return tuple((b + base, m) for b, m in spans)
+        def finish_out(b, m, acc):
+            own = x0[pl.ds((3 + b) * w, m * w), c : 2 * c].astype(F32)
+            outb[t, pl.ds(b * w, m * w)] = (own + (acc + bias[2])).astype(BF16)
 
         if t == 0:
             @pl.when(decoder)
@@ -265,12 +249,10 @@
             bias_copy.wait()
             k_copies[0].wait()
         a_end = q + h - 2
-        first = ((1, a_end),)
-        second = ((1 + a_end, rows - 2 - a_end),)
-        step(x0, spans_at(first, 2), 0, store(x1, 2, first))
+        step(x0, 2, ((1, a_end),), 0, store(x1, 2, 0))
         arrived(3)
         put(x0, 3 + pieces[3][0], joined(3).astype(F32))
-        step(x0, spans_at(second, 2), 0, store(x1, 2, second))
+        step(x0, 2, ((1 + a_end, rows - 2 - a_end),), 0, store(x1, 2, 0))
 
         @pl.when(has_down)
         def _():
@@ -282,22 +264,21 @@
 
         put(x0, 0, halo[t, 0].astype(F32))
         put(x0, 3 + rows, halo[t, 1].astype(F32))
-        edge1 = ((-2, 3), (rows - 1, 3))
-        step(x0, spans_at(edge1, 2), 0, store(x1, 2, edge1, 2))
+        step(x0, 2, ((-2, 3), (rows - 1, 3)), 0, store(x1, 2, 0))
         if t == 0:
             k_copies[1].wait()
-        ring2 = ((2, 3), (rows - 5, 3))
-        step(x1, spans_at(ring2, 1), 1, store(x2, 1, ring2))
-        edge2 = ((-1, 3), (rows - 2, 3))
-        step(x1, spans_at(edge2, 1), 1, store(x2, 1, edge2, 1))
-        core2 = ((5, rows - 10),)
-        step(x1, spans_at(core2, 1), 1, store(x2, 1, core2))
+        step(x1, 1, ((5, rows - 10),), 1, store(x2, 1, 1))
+        step(x1, 1, ((-1, 6), (rows - 5, 6)), 1, store(x2, 1, 1))
         if t == 0:
             k_copies[2].wait()
-        ends = (pieces[0], pieces[1])
-        step(x2, ends, 2, result(ends, (0, 1)))
+        step(x2, 0, (pieces[0], pieces[1]), 2, finish_out)
+        flush()
+        emit(0)
+        emit(1)
         for p in (2, 3):
-            step(x2, (pieces[p],), 2, result((pieces[p],), (p,)))
+            step(x2, 0, (pieces[p],), 2, finish_out)
+            flush()
+            emit(p)
         flush()
         pltpu.make_async_copy(outb.at[t], maps.at[t], out_s.at[t]).start()
 

time: 58 us -> 54.5 us (0.940)
  Pallas kernels: 53.2 us -> 49.3 us
    pallas_call x1, Pallas kernels: 53.2 us -> 49.3 us  [on_device(): pl.pallas_call(functools.partial(body, ticks, rows, w, c), out_shape=(sha...]
where the time goes in v3:
time: 54.5 us; the launch traced here: 53.9 us
  Pallas kernels  49.3 us (90%)
  other arithmetic  2.78 us (5%)
  local copies, waits for them, and re-layouts  1.15 us (2%)
  between operations  0.65 us (1%)
    pallas_call x1, Pallas kernels, on_device(): pl.pallas_call(functools.partial(body, ticks, rows, w, c), out_shape=(sha...  49.3 us
    select_n x1, other arithmetic, on_device(): stash = jnp.where(decoder, stash, jnp.zeros_like(stash))  2.78 us
    unnamed x3, local copies, waits for them, and re-layouts  1.15 us

profile of v3, /device:TPU:13, one launch (start us, length us, event | category | flops | bytes accessed | tf_op | source)
XLA Modules:
  0.0 53.9 jit_solution(11253770289648834488)
XLA Ops:
  0.6 49.3 %shard_map.68 = (bf16[3,1024,256]{2,1,0:T(8,128)(2,1)}, bf16[3,1024,256]{2,1,0:T(8,128)(2,1)}) custom-call(bf16[1024,256]{1,0:T(8,128)(2,1)} %bitcast.16, bf16[3,1024,256]{2,1,0:T(8,128)(2,1)} %bitcast.13, bf16[3,1024,256]{2,1,0:T(8,128)(2,1)} %bitcast.14, bf16[3,2304,256]{2,1,0:T(8,128)(2,1)} %bitcast.11, f32[3,1,256]{2,1,0:T(1,128)} %bitcast.17), custom_call_target="tpu_custom_call" | custom-call | tf_op jit(solution)/shard_map/pallas_call | solution.py:328
  50.0 0.0 copy-start
  50.0 2.8 %broadcast_select_fusion = bf16[3,1024,256]{2,1,0:T(8,128)(2,1)} fusion(bf16[3,1024,256]{2,1,0:T(8,128)(2,1)} %get-tuple-element.5, pred[]{:T(512)S(6)} %ge.3), kind=kLoop, calls=%fused_computation | loop fusion | flops 786432 | bytes 3145729 | tf_op jit(solution)/shard_map/jit(_where)/select_n | solution.py:367
  52.7 0.0 copy-done
  52.8 1.1 %copy.10 = bf16[3,1,16,64,256]{4,3,2,1,0:T(8,128)(2,1)} copy(bf16[3,1,16,64,256]{4,3,2,1,0:T(8,128)(2,1)S(1)} %bitcast.12) | data formatting | bytes 3145728
Async XLA Ops:
  50.0 2.8 %copy-start = (bf16[3,1024,256]{2,1,0:T(8,128)(2,1)S(1)}, bf16[3,1024,256]{2,1,0:T(8,128)(2,1)}, u32[]{:S(2)}) copy-start(bf16[3,1024,256]{2,1,0:T(8,128)(2,1)} %get-tuple-element.4) | copy-start | bytes 4718596
